TPU v7x, 32 devices: a whole 2x2x4 slice. The times are simulated.
32 devices in a mesh: tilt: 2 (over y), dom: 16 (over z, x, core).
Axes of the slice: x: 2, y: 2, z: 4, core: 2. Of those that a mesh axis runs over, the one named last changes fastest.
Arguments:
- sections: bfloat16 [32, 256, 256], P('dom'), may hold values from -6 to 6
- images: bfloat16 [32, 4, 256, 256], P('dom', 'tilt'), may hold values from -6 to 6
- slice_rows: bfloat16 [4, 256, 256], P('tilt'), may hold values from -0.375 to 0.375
- slice_cols: bfloat16 [4, 256, 256], P('tilt'), may hold values from -0.375 to 0.375
- ctf_filter: bfloat16 [4, 256, 256], P('tilt'), may hold values from -0.375 to 0.375
- nbr_owner: int32 [32, 2, 8], P('dom'), may hold values from 0 to 15, all different within a row; in each aligned block of 4 rows (0 to 3, 4 to 7, ..., all dimensions but the last counted through in order) at most 4 rows name the same one
- nbr_local: int32 [32, 16], P('dom'), may hold values from 0 to 1
- nbr_side: int32 [32, 16], P('dom'), may hold values from 0 to 1
- nbr_weight: float32 [32, 16], P('dom'), may hold values from 0.25 to 2
Outputs:
- section_grad: float32 [32, 256, 256], P('dom', 'tilt')
- scores: float32 [32], P('dom')
Inputs may be any that keep to these rules, and one draw needn't show every extreme that they name: `nbr_owner`: among the 32 neighbour entries of one spatial block's particles, at most 4 name the same owner block; some blocks reach 4.
All inputs are finite; a program needn't handle non-finite values.
Results may differ from a plain program's by a relative error of at most 0.013.
Values may be sent and summed in bfloat16 or wider, within the bound.
No kernel may reach another device: no remote copies, remote signals or barrier semaphores. Data moves between devices by JAX's collectives and lax.ppermute only.
A program may use at most 64 MiB of HBM per device.

v0:
```python
import jax
import jax.numpy as jnp
from jax import lax
from jax.sharding import PartitionSpec as P

OVL = 16


def split_dot(weights, bands):
    hi = weights.astype(jnp.bfloat16)
    rest = weights - hi.astype(jnp.float32)
    mid = rest.astype(jnp.bfloat16)
    low = (rest - mid.astype(jnp.float32)).astype(jnp.bfloat16)
    total = jnp.dot(hi, bands, preferred_element_type=jnp.float32)
    total = total + jnp.dot(mid, bands, preferred_element_type=jnp.float32)
    return total + jnp.dot(low, bands, preferred_element_type=jnp.float32)


def on_device(
    sections, images, slice_rows, slice_cols, ctf_filter, nbr_owner, nbr_local, nbr_side, nbr_weight
):
    own_count = sections.shape[0]
    pixels = sections.shape[1]
    tilt_count = images.shape[1]
    neighbours = nbr_local.shape[1]
    peer_count = lax.axis_size("dom")
    total = own_count * peer_count
    me = lax.axis_index("dom")
    band_size = tilt_count * OVL * pixels
    target = nbr_owner.reshape(own_count, neighbours) * own_count + nbr_local
    every = jnp.arange(total)
    hits = target[:, :, None] == every[None, None, :]
    fwd = [
        jnp.sum(jnp.where(hits & (nbr_side == s)[:, :, None], nbr_weight[:, :, None], 0.0), axis=1)
        for s in (0, 1)
    ]
    target_all = lax.all_gather(target, "dom", axis=0, tiled=True)
    side_all = lax.all_gather(nbr_side, "dom", axis=0, tiled=True)
    weight_all = lax.all_gather(nbr_weight, "dom", axis=0, tiled=True)
    halfway = jnp.einsum(
        "kij,tlj->ktil", sections, slice_cols, preferred_element_type=jnp.float32
    ).astype(jnp.bfloat16)
    projected = jnp.einsum(
        "tai,ktil->ktal", slice_rows, halfway, preferred_element_type=jnp.float32
    ).astype(jnp.bfloat16)
    edges = jnp.stack((projected[:, :, :OVL], projected[:, :, pixels - OVL :]), axis=1)
    edges_all = lax.all_gather(edges, "dom", axis=0, tiled=True)
    lower_part = split_dot(fwd[0], edges_all[:, 0].reshape(total, band_size))
    upper_part = split_dot(fwd[1], edges_all[:, 1].reshape(total, band_size))
    lower_part = lower_part.reshape(own_count, tilt_count, OVL, pixels)
    upper_part = upper_part.reshape(own_count, tilt_count, OVL, pixels)
    residual = images.astype(jnp.float32) - projected.astype(jnp.float32)
    residual = residual.at[:, :, :OVL].add(-upper_part)
    residual = residual.at[:, :, pixels - OVL :].add(-lower_part)
    residual_portion = residual.astype(jnp.bfloat16)
    smoothed_images = jnp.einsum(
        "tab,ktbc->ktac", ctf_filter, residual_portion, preferred_element_type=jnp.float32
    ).astype(jnp.bfloat16)
    filtered_images = jnp.einsum(
        "ktac,tdc->ktad", smoothed_images, ctf_filter, preferred_element_type=jnp.float32
    )
    score_part = jnp.sum(filtered_images * filtered_images, axis=(1, 2, 3))
    tilt_groups = lax.axis_size("tilt")
    scores = 0.5 * lax.psum(score_part, "tilt") / (tilt_count * tilt_groups * pixels * pixels)
    filtered_portion = filtered_images.astype(jnp.bfloat16)
    reverse_pass = jnp.einsum(
        "tab,ktac->ktbc", ctf_filter, filtered_portion, preferred_element_type=jnp.float32
    ).astype(jnp.bfloat16)
    weighted = jnp.einsum(
        "ktbc,tcd->ktbd", reverse_pass, ctf_filter, preferred_element_type=jnp.float32
    ).astype(jnp.bfloat16)
    grad_bands = jnp.stack((weighted[:, :, :OVL], weighted[:, :, pixels - OVL :]), axis=1)
    grad_all = lax.all_gather(grad_bands, "dom", axis=0, tiled=True)
    mine = me * own_count + jnp.arange(own_count)
    named = target_all[None, :, :] == mine[:, None, None]
    back = [
        jnp.sum(jnp.where(named & (side_all == s)[None], weight_all[None], 0.0), axis=2)
        for s in (0, 1)
    ]
    add_top = split_dot(back[0], grad_all[:, 1].reshape(total, band_size))
    add_bottom = split_dot(back[1], grad_all[:, 0].reshape(total, band_size))
    add_top = add_top.reshape(own_count, tilt_count, OVL, pixels)
    add_bottom = add_bottom.reshape(own_count, tilt_count, OVL, pixels)
    proj_grad = weighted.astype(jnp.float32)
    proj_grad = proj_grad.at[:, :, :OVL].add(add_top)
    proj_grad = proj_grad.at[:, :, pixels - OVL :].add(add_bottom)
    proj_half = proj_grad.astype(jnp.bfloat16)
    upward = jnp.einsum(
        "tai,ktal->ktil", slice_rows, proj_half, preferred_element_type=jnp.float32
    ).astype(jnp.bfloat16)
    partial_grad = -jnp.einsum(
        "ktil,tlj->kij", upward, slice_cols, preferred_element_type=jnp.float32
    )
    section_grad = lax.psum_scatter(partial_grad, "tilt", scatter_dimension=1, tiled=True)
    return (section_grad, scores)


def solution(mesh):
    in_specs = (
        P("dom", None, None),
        P("dom", "tilt", None, None),
        P("tilt", None, None),
        P("tilt", None, None),
        P("tilt", None, None),
        P("dom", None, None),
        P("dom", None),
        P("dom", None),
        P("dom", None),
    )
    out_specs = (P("dom", "tilt", None), P("dom"))
    return jax.shard_map(
        on_device, mesh=mesh, in_specs=in_specs, out_specs=out_specs, check_vma=False
    )
```

profile of v0, /device:TPU:0, one launch (start us, length us, event | category | flops | bytes accessed | tf_op | source)
XLA Modules:
  0.0 136.8 jit_solution(1483881849874437)
XLA Ops:
  7.2 0.0 copy-start
  7.2 0.0 all-gather.6.cloned.1.call-start
  7.2 1.9 %convert_subtract_fusion = (f32[2,2,256,256]{3,2,0,1:T(8,128)S(1)}, bf16[2,2,256,256]{3,2,0,1:T(8,128)(2,1)S(1)}) fusion(bf16[2,2,256,256]{3,2,1,0:T(8,128)(2,1)} %param.18, bf16[2,256,256]{2,1,0:T(8,128)(2,1)} %param.19, bf16[2,256,256]{2,1,0:T(8,128)(2,1)} %param.20, bf16[2,256,256]{2,1,0:T(8,128)(2,1)} %param.17), kind=kOutput, calls=%fused_computation.26 | convolution fusion | flops 269746176 | bytes 2883584 | tf_op jit(solution)/shard_map/tai,ktil->ktal/dot_general | solution.py:43
  9.1 0.6 pad_maximum_fusion
  9.7 0.0 copy-start.5
  9.7 0.0 all-gather.6.cloned.1.call-update
  9.8 0.0 all-gather.8.cloned.1.call-start
  9.8 0.6 copy-done.5
  10.4 0.0 copy-start.6
  10.4 0.1 mul.19
  10.5 0.6 copy-done.6
  11.1 0.0 copy-start.4
  11.1 0.7 copy-done.4
  11.8 0.0 copy-start.3
  11.8 0.7 copy-done.3
  12.5 0.1 select_reduce_fusion.2
  12.6 38.9 %all-gather.6.cloned.1.call-done = bf16[32,2,2,16,256]{4,3,0,2,1:T(8,128)(2,1)} async-done(((bf16[2,2,2,16,256]{4,3,0,2,1:T(8,128)(2,1)}), bf16[32,2,2,16,256]{4,3,0,2,1:T(8,128)(2,1)}) %all-gather.6.cloned.1.call-update) | async-done | bytes 1048592 | tf_op jit(solution)/shard_map/all_gather | solution.py:47
  51.5 1.3 fusion.53
  52.7 0.1 copy.39
  52.8 0.2 reshape_squeeze.12
  53.1 0.2 fusion.37
  53.2 0.2 convolution_add_fusion.7
  53.4 0.2 fusion.1
  53.6 0.1 copy.41
  53.7 0.2 reshape_squeeze.13
  54.0 0.2 fusion.41
  54.1 0.2 convolution_add_fusion.5
  54.3 0.2 fusion
  54.6 0.0 copy-done
  54.6 0.7 multiply_reduce_fusion
  55.3 0.6 fusion.58
  55.9 0.6 pad_maximum_fusion.1
  56.6 0.0 all-gather.8.cloned.1.call-update
  56.6 0.0 reduce-scatter.2.cloned.1.call-start
  56.7 19.3 %all-gather.2 = f32[16,2,16]{2,1,0:T(2,128)S(1)} all-gather(f32[1,2,16]{2,1,0:T(2,128)S(1)} %bitcast.146), channel_id=1, replica_groups=mesh['tilt'=2,'dom'=16] {'dom'}, dimensions={0}, use_global_device_ids=true | all-gather | bytes 2176 | tf_op jit(solution)/shard_map/all_gather | solution.py:39
  76.0 0.1 copy.49
  76.1 17.4 %all-gather = s32[16,2,16]{2,1,0:T(2,128)S(1)} all-gather(s32[1,2,16]{2,1,0:T(2,128)S(1)} %bitcast.145), channel_id=1, replica_groups=mesh['tilt'=2,'dom'=16] {'dom'}, dimensions={0}, use_global_device_ids=true | all-gather | bytes 2176 | tf_op jit(solution)/shard_map/all_gather | solution.py:37
  93.5 0.1 copy.47
  93.5 18.8 %all-gather.1 = s32[16,2,16]{2,1,0:T(2,128)S(1)} all-gather(s32[1,2,16]{2,1,0:T(2,128)S(1)} %bitcast.147), channel_id=1, replica_groups=mesh['tilt'=2,'dom'=16] {'dom'}, dimensions={0}, use_global_device_ids=true | all-gather | bytes 2176 | tf_op jit(solution)/shard_map/all_gather | solution.py:38
  112.4 0.1 copy.52
  112.5 0.1 copy.48
  112.6 0.1 select_reduce_fusion
  112.7 0.0 all-gather.8.cloned.1.call-done
  112.7 1.3 fusion.52
  114.0 0.1 copy.50
  114.0 0.2 reshape_squeeze.14
  114.3 0.2 fusion.45
  114.5 0.2 convolution_add_fusion.3
  114.7 0.2 convolution_add_fusion.2
  114.9 0.1 copy.53
  114.9 0.2 reshape_squeeze.15
  115.2 0.2 fusion.49
  115.4 0.2 convolution_add_fusion.1
  115.6 0.2 convolution_add_fusion
  115.8 0.0 copy-start.1
  115.8 0.0 copy-start.2
  115.9 0.9 copy-done.1
  116.7 0.1 copy-done.2
  116.8 1.5 %fusion.9 = f32[2,256,256]{2,1,0:T(8,128)} fusion(bf16[2,256,256]{2,1,0:T(8,128)(2,1)S(1)} %copy-done.1, bf16[2,256,256]{2,1,0:T(8,128)(2,1)S(1)} %copy-done.2, f32[2,2,256,256]{3,2,0,1:T(8,128)S(1)} %fusion.30), kind=kOutput, calls=%fused_computation.24 | convolution fusion | flops 269090816 | bytes 2097152 | tf_op jit(solution)/shard_map/ktil,tlj->kij/dot_general | solution.py:91
  118.3 0.0 reduce-scatter.2.cloned.1.call-update
  118.3 4.9 %psum.7 = f32[2]{0:T(128)S(1)} all-reduce(f32[2]{0:T(128)S(1)} %get-tuple-element.70), channel_id=1, replica_groups=mesh['tilt'=2,'dom'=16] {'tilt'}, use_global_device_ids=true, to_apply=%region_6.7 | all-reduce | flops 2 | bytes 16 | tf_op jit(solution)/shard_map/psum | solution.py:64
  123.3 0.5 broadcast_multiply_fusion.1
  123.8 6.5 %reduce-scatter.2.cloned.1.call-done = f32[2,128,256]{2,1,0:T(8,128)} async-done(((f32[2,256,256]{2,1,0:T(8,128)}), f32[2,128,256]{2,1,0:T(8,128)}) %reduce-scatter.2.cloned.1.call-update) | async-done | bytes 262160 | tf_op jit(solution)/shard_map/reduce_scatter | solution.py:94
  (17 shorter events, 0.2 us)
Async XLA Ops:
  7.2 47.4 %copy-start = (bf16[2,256,256]{2,1,0:T(8,128)(2,1)S(1)}, bf16[2,256,256]{2,1,0:T(8,128)(2,1)}, u32[]{:S(2)}) copy-start(bf16[2,256,256]{2,1,0:T(8,128)(2,1)} %param.21) | copy-start | bytes 786436
  7.2 44.3 %all-gather.6.cloned.1.call-start = ((), (), s32[]{:S(2)}) async-start(), calls=%async_computation.1 | async-start | bytes 1114112 | tf_op jit(solution)/shard_map/all_gather | solution.py:47
  9.7 0.7 copy-start.5
  9.8 102.9 %all-gather.8.cloned.1.call-start = ((), (), s32[]{:S(2)}) async-start(), calls=%async_computation.2 | async-start | bytes 1114112 | tf_op jit(solution)/shard_map/all_gather | solution.py:73
  10.4 0.7 copy-start.6
  11.1 0.7 copy-start.4
  11.8 0.7 copy-start.3
  56.6 73.7 %reduce-scatter.2.cloned.1.call-start = ((), (), s32[]{:S(2)}) async-start(), calls=%async_computation.3 | async-start | bytes 786432 | tf_op jit(solution)/shard_map/reduce_scatter | solution.py:94
  115.8 1.0 copy-start.1
  115.8 1.0 copy-start.2
Sparse Core Ops, SparseCore 0:
  10.8 40.6 all-gather.5
  56.7 36.8 all-gather.7
  118.5 11.8 reduce-scatter.1
where the time goes:
time: 137 us
  blocking collectives  60.5 us (44%)
  waiting for transfers between devices  45.5 us (33%)
  between operations  14 us (10%)
  local copies, waits for them, and re-layouts  7.73 us (6%)
  matrix products  6.92 us (5%)
  other arithmetic  2.08 us (2%)
    all_gather x1, waiting for transfers between devices, on_device(): edges_all = lax.all_gather(edges, 'dom', axis=0, tiled=True)  38.9 us
    all_gather x1, blocking collectives, on_device(): weight_all = lax.all_gather(nbr_weight, 'dom', axis=0, tiled=True)  19.3 us
    all_gather x1, blocking collectives, on_device(): side_all = lax.all_gather(nbr_side, 'dom', axis=0, tiled=True)  18.8 us
    all_gather x1, blocking collectives, on_device(): target_all = lax.all_gather(target, 'dom', axis=0, tiled=True)  17.4 us
    reduce_scatter x1, waiting for transfers between devices, on_device(): lax.psum_scatter(partial_grad, 'tilt', scatter_dimension=1, tiled=True)  6.51 us
    psum x1, blocking collectives, on_device(): lax.psum(score_part, 'tilt')  4.94 us
    unnamed x20, local copies, waits for them, and re-layouts  3.68 us
  transfers between devices with their start and end apart: 3, of which 2 were waited for; matrix products, arithmetic and copies ran while one was open for 1% of the time, Pallas kernels for 0%

commit v1 on v0

--- a/solution.py
+++ b/solution.py
@@ -2,8 +2,16 @@
 import jax.numpy as jnp
 from jax import lax
 from jax.sharding import PartitionSpec as P
+from jax.lax import all_gather
 
 OVL = 16
+
+
+def search_point(ax_name, x_local, values):
+    clean = jnp.concatenate([x_local, values], axis=1)
+    a_now = all_gather(clean, axis_name=ax_name, tiled=True, axis=0)
+    mixed_arr = jnp.split(a_now, [x_local.shape[1]], axis=1)
+    return mixed_arr
 
 
 def split_dot(weights, bands):
@@ -35,8 +43,7 @@
         for s in (0, 1)
     ]
     target_all = lax.all_gather(target, "dom", axis=0, tiled=True)
-    side_all = lax.all_gather(nbr_side, "dom", axis=0, tiled=True)
-    weight_all = lax.all_gather(nbr_weight, "dom", axis=0, tiled=True)
+    side_all, weight_all = search_point("dom", nbr_side, nbr_weight)
     halfway = jnp.einsum(
         "kij,tlj->ktil", sections, slice_cols, preferred_element_type=jnp.float32
     ).astype(jnp.bfloat16)

time: 137 us -> 120 us (0.88)
  blocking collectives: 60.5 us -> 41.7 us
  waiting for transfers between devices: 45.5 us -> 46.9 us
    all_gather x2 -> x1, blocking collectives: 38.1 us -> 19.3 us  [search_point(): a_now = all_gather(clean, axis_name=ax_name, tiled=True, axis=0)]
    reduce_scatter x1, waiting for transfers between devices: 6.51 us -> 7.94 us  [on_device(): lax.psum_scatter(partial_grad, 'tilt', scatter_dimension=1, tiled=True)]
where the time goes in v1:
time: 120 us; the launch traced here: 119 us
  waiting for transfers between devices  46.9 us (39%)
  blocking collectives  41.7 us (35%)
  between operations  14 us (12%)
  local copies, waits for them, and re-layouts  7.66 us (6%)
  matrix products  6.92 us (6%)
  other arithmetic  2.15 us (2%)
    all_gather x1, waiting for transfers between devices, on_device(): edges_all = lax.all_gather(edges, 'dom', axis=0, tiled=True)  38.9 us
    all_gather x1, blocking collectives, search_point(): a_now = all_gather(clean, axis_name=ax_name, tiled=True, axis=0)  19.3 us
    all_gather x1, blocking collectives, on_device(): target_all = lax.all_gather(target, 'dom', axis=0, tiled=True)  17.4 us
    reduce_scatter x1, waiting for transfers between devices, on_device(): lax.psum_scatter(partial_grad, 'tilt', scatter_dimension=1, tiled=True)  7.94 us
    psum x1, blocking collectives, on_device(): lax.psum(score_part, 'tilt')  4.94 us
    unnamed x20, local copies, waits for them, and re-layouts  3.68 us
  transfers between devices with their start and end apart: 3, of which 2 were waited for; matrix products, arithmetic and copies ran while one was open for 1% of the time, Pallas kernels for 0%

profile of v1, /device:TPU:0, one launch (start us, length us, event | category | flops | bytes accessed | tf_op | source)
XLA Modules:
  0.0 119.5 jit_solution(6900480966023531452)
XLA Ops:
  7.2 0.0 copy-start
  7.2 0.0 all-gather.5.cloned.1.call-start
  7.2 1.9 %convert_subtract_fusion = (f32[2,2,256,256]{3,2,0,1:T(8,128)S(1)}, bf16[2,2,256,256]{3,2,0,1:T(8,128)(2,1)S(1)}) fusion(bf16[2,2,256,256]{3,2,1,0:T(8,128)(2,1)} %param.18, bf16[2,256,256]{2,1,0:T(8,128)(2,1)} %param.19, bf16[2,256,256]{2,1,0:T(8,128)(2,1)} %param.20, bf16[2,256,256]{2,1,0:T(8,128)(2,1)} %param.17), kind=kOutput, calls=%fused_computation.26 | convolution fusion | flops 269746176 | bytes 2883584 | tf_op jit(solution)/shard_map/tai,ktil->ktal/dot_general | solution.py:50
  9.1 0.6 pad_maximum_fusion
  9.7 0.0 copy-start.5
  9.7 0.0 all-gather.5.cloned.1.call-update
  9.8 0.0 all-gather.7.cloned.1.call-start
  9.8 0.6 copy-done.5
  10.4 0.0 copy-start.6
  10.4 0.1 mul.19
  10.5 0.6 copy-done.6
  11.1 0.0 copy-start.4
  11.1 0.7 copy-done.4
  11.8 0.0 copy-start.3
  11.8 0.7 copy-done.3
  12.5 0.1 select_reduce_fusion.2
  12.6 38.9 %all-gather.5.cloned.1.call-done = bf16[32,2,2,16,256]{4,3,0,2,1:T(8,128)(2,1)} async-done(((bf16[2,2,2,16,256]{4,3,0,2,1:T(8,128)(2,1)}), bf16[32,2,2,16,256]{4,3,0,2,1:T(8,128)(2,1)}) %all-gather.5.cloned.1.call-update) | async-done | bytes 1048592 | tf_op jit(solution)/shard_map/all_gather | solution.py:54
  51.5 1.3 %fusion.53 = (bf16[32,1,2,16,256]{4,3,0,2,1:T(8,128)(2,1)S(1)}, bf16[32,1,2,16,256]{4,3,0,2,1:T(8,128)(2,1)S(1)}) fusion(bf16[32,2,2,16,256]{4,3,0,2,1:T(8,128)(2,1)} %all-gather.5.cloned.1.call-done), kind=kLoop, calls=%fused_computation.90 | loop fusion | bytes 2097152 | tf_op jit(solution)/shard_map/slice | solution.py:55
  52.7 0.1 copy.77
  52.8 0.2 reshape_squeeze.12
  53.1 0.2 fusion.37
  53.2 0.2 convolution_add_fusion.7
  53.4 0.2 fusion.1
  53.6 0.1 copy.79
  53.7 0.2 reshape_squeeze.13
  54.0 0.2 fusion.41
  54.1 0.2 convolution_add_fusion.5
  54.3 0.2 fusion
  54.6 0.0 copy-done
  54.6 0.7 multiply_reduce_fusion
  55.3 0.6 fusion.59
  55.9 0.6 pad_maximum_fusion.1
  56.6 0.0 all-gather.7.cloned.1.call-update
  56.6 0.0 reduce-scatter.2.cloned.1.call-start
  56.7 0.1 maximum_bitcast_fusion
  56.7 19.3 %all-gather.1 = f32[16,2,32]{2,1,0:T(2,128)S(1)} all-gather(f32[1,2,32]{2,1,0:T(2,128)S(1)} %maximum_bitcast_fusion), channel_id=1, replica_groups=mesh['tilt'=2,'dom'=16] {'dom'}, dimensions={0}, use_global_device_ids=true | all-gather | bytes 4352 | tf_op jit(solution)/shard_map/all_gather | solution.py:12
  76.1 0.1 fusion.54
  76.1 0.1 copy.87
  76.2 17.4 %all-gather = s32[16,2,16]{2,1,0:T(2,128)S(1)} all-gather(s32[1,2,16]{2,1,0:T(2,128)S(1)} %bitcast.145), channel_id=1, replica_groups=mesh['tilt'=2,'dom'=16] {'dom'}, dimensions={0}, use_global_device_ids=true | all-gather | bytes 2176 | tf_op jit(solution)/shard_map/all_gather | solution.py:45
  93.6 0.1 copy.85
  93.7 0.1 copy.106
  93.8 0.1 select_reduce_fusion
  93.9 0.0 all-gather.7.cloned.1.call-done
  93.9 1.3 %fusion.52 = (bf16[32,1,2,16,256]{4,3,0,2,1:T(8,128)(2,1)S(1)}, bf16[32,1,2,16,256]{4,3,0,2,1:T(8,128)(2,1)S(1)}) fusion(bf16[32,2,2,16,256]{4,3,0,2,1:T(8,128)(2,1)} %all-gather.7.cloned.1.call-done), kind=kLoop, calls=%fused_computation.89 | loop fusion | bytes 2097152 | tf_op jit(solution)/shard_map/slice | solution.py:88
  95.2 0.1 copy.88
  95.2 0.2 reshape_squeeze.14
  95.5 0.2 fusion.45
  95.7 0.2 convolution_add_fusion.3
  95.9 0.2 convolution_add_fusion.2
  96.1 0.1 copy.90
  96.1 0.2 reshape_squeeze.15
  96.4 0.2 fusion.49
  96.6 0.2 convolution_add_fusion.1
  96.8 0.2 convolution_add_fusion
  97.0 0.0 copy-start.1
  97.0 0.0 copy-start.2
  97.0 0.9 copy-done.1
  97.9 0.1 copy-done.2
  98.0 1.5 %fusion.9 = f32[2,256,256]{2,1,0:T(8,128)} fusion(bf16[2,256,256]{2,1,0:T(8,128)(2,1)S(1)} %copy-done.1, bf16[2,256,256]{2,1,0:T(8,128)(2,1)S(1)} %copy-done.2, f32[2,2,256,256]{3,2,0,1:T(8,128)S(1)} %fusion.30), kind=kOutput, calls=%fused_computation.24 | convolution fusion | flops 269090816 | bytes 2097152 | tf_op jit(solution)/shard_map/ktil,tlj->kij/dot_general | solution.py:98
  99.5 0.0 reduce-scatter.2.cloned.1.call-update
  99.5 4.9 %psum.7 = f32[2]{0:T(128)S(1)} all-reduce(f32[2]{0:T(128)S(1)} %get-tuple-element.72), channel_id=1, replica_groups=mesh['tilt'=2,'dom'=16] {'tilt'}, use_global_device_ids=true, to_apply=%region_6.7 | all-reduce | flops 2 | bytes 16 | tf_op jit(solution)/shard_map/psum | solution.py:71
  104.5 0.5 broadcast_multiply_fusion.1
  105.0 7.9 %reduce-scatter.2.cloned.1.call-done = f32[2,128,256]{2,1,0:T(8,128)} async-done(((f32[2,256,256]{2,1,0:T(8,128)}), f32[2,128,256]{2,1,0:T(8,128)}) %reduce-scatter.2.cloned.1.call-update) | async-done | bytes 262160 | tf_op jit(solution)/shard_map/reduce_scatter | solution.py:101
  (16 shorter events, 0.1 us)
Async XLA Ops:
  7.2 47.4 %copy-start = (bf16[2,256,256]{2,1,0:T(8,128)(2,1)S(1)}, bf16[2,256,256]{2,1,0:T(8,128)(2,1)}, u32[]{:S(2)}) copy-start(bf16[2,256,256]{2,1,0:T(8,128)(2,1)} %param.21) | copy-start | bytes 786436
  7.2 44.3 %all-gather.5.cloned.1.call-start = ((), (), s32[]{:S(2)}) async-start(), calls=%async_computation.1 | async-start | bytes 1114112 | tf_op jit(solution)/shard_map/all_gather | solution.py:54
  9.7 0.7 copy-start.5
  9.8 84.1 %all-gather.7.cloned.1.call-start = ((), (), s32[]{:S(2)}) async-start(), calls=%async_computation.2 | async-start | bytes 1114112 | tf_op jit(solution)/shard_map/all_gather | solution.py:80
  10.4 0.7 copy-start.6
  11.1 0.7 copy-start.4
  11.8 0.7 copy-start.3
  56.6 56.3 %reduce-scatter.2.cloned.1.call-start = ((), (), s32[]{:S(2)}) async-start(), calls=%async_computation.3 | async-start | bytes 786432 | tf_op jit(solution)/shard_map/reduce_scatter | solution.py:101
  97.0 1.0 copy-start.1
  97.0 1.0 copy-start.2
Sparse Core Ops, SparseCore 0:
  10.8 40.6 all-gather.4
  56.7 36.8 all-gather.6
  99.7 13.2 reduce-scatter.1
